TPU v7x, 128 devices: a whole 4x4x4 slice. The times are simulated.
128 devices in a mesh: gx: 8 (over y, core), gy: 8 (over x, z_hi), ga: 2 (over z_lo).
Axes of the slice: x: 4, y: 4, z: 4 (z_hi: 2, z_lo: 2; z = z_hi * 2 + z_lo), core: 2. Of those that a mesh axis runs over, the one named last changes fastest.
Arguments:
- offsets: float32 [3, 16, 16, 32, 128], P(None, 'gx', 'gy', 'ga'), may hold values from 0 to 1
- charge: float32 [16, 16, 32, 128], P('gx', 'gy', 'ga'), may hold values from -3 to 3
- counts: int32 [16, 16, 32], P('gx', 'gy', 'ga'), may hold values from 8 to 128, as said below
- partners: int32 [16, 16, 32, 128], P('gx', 'gy', 'ga'), may hold values from 0 to 127
Outputs:
- short_force: float32 [3, 16, 16, 32, 128], P(None, 'gx', 'gy', 'ga')
- long_force: float32 [3, 16, 16, 32, 128], P(None, 'gx', 'gy', 'ga')
Inputs may be any that keep to these rules, and one draw needn't show every extreme that they name: `counts`: each cell holds at least 8 beads and at most 128; some cell holds exactly 128.
All inputs are finite; a program needn't handle non-finite values.
Results may differ from a plain program's by a relative error of at most 0.0003.
Values sent between devices are 32-bit elements; how exact they have to be, the bound alone decides.
No kernel may reach another device: no remote copies, remote signals or barrier semaphores. Data moves between devices by JAX's collectives and lax.ppermute only.
A program may use at most 192 MiB of HBM per device.

v0:
```python
import jax
import jax.numpy as jnp
import numpy as np
from jax import lax
from jax.experimental import pallas as pl
from jax.experimental.pallas import tpu as pltpu
from jax.sharding import PartitionSpec as P

f32, bf16, i32 = jnp.float32, jnp.bfloat16, jnp.int32
LAST = (((1,), (1,)), ((), ()))
CAP = 65.0 / 64.0
TILES = 2
INNER, OUTER = (128, 8, 4), (64, 16, 1)
VMEM = pl.BlockSpec(memory_space=pltpu.VMEM)
SMEM = pl.BlockSpec(memory_space=pltpu.SMEM)
ANY = pl.BlockSpec(memory_space=pl.ANY)


def fine_kernel(gap):
    return np.where(np.abs(gap) <= 8, np.exp(-gap * gap / 12.5), 0.0)


def coarse_kernel(gap):
    return np.where(np.abs(gap) <= 8, np.exp(-gap * gap / 72.0), 0.0)


def hat(gap):
    return np.where(gap == 0, 1.0, np.where(np.abs(gap) == 1, 0.5, 0.0))


def halves(matrix):
    high = matrix.astype(np.float32).astype(jnp.bfloat16)
    low = (matrix - high.astype(np.float64)).astype(np.float32).astype(jnp.bfloat16)
    return high, low


def z_operator(part):
    source = np.full(256, 10**6, np.int64)
    source[:131] = 128 * part - 1 + np.arange(131)
    source[160:181] = np.arange(21) + (127 if part == 0 else 109)
    inside = (source >= 0) & (source < 256)
    result = np.zeros((256, 256))
    target = 128 * part - 1 + np.arange(131)
    fine = fine_kernel((target[None, :] - source[:, None]).astype(np.float64))
    result[:, :131] = fine * ((target >= 0) & (target < 256))[None, :]
    middle = np.arange(128)
    down = hat((source[:, None] - 2 * middle[None, :]).astype(np.float64))
    point = 64 * part - 1 + np.arange(67)
    spread = coarse_kernel((middle[:, None] - point[None, :]).astype(np.float64))
    spread = spread * ((point >= 0) & (point < 128))[None, :]
    result[:, 136:203] = down @ spread
    return result * inside[:, None]


def y_operators():
    fines, coarses = [], []
    for place in range(4):
        near, far = (1 - 2 * (place & 1)), (1 - (place & 2))
        parts = [np.where(np.arange(24) < 19, np.arange(24), 10**6)]
        for side in (near, -near):
            parts.append(np.where(np.arange(16) < 11, np.arange(16) + (16 if side > 0 else -8), 10**6))
        fine = fine_kernel(np.arange(24)[:, None] - np.concatenate(parts)[None, :].astype(np.float64))
        fine[19:] = 0
        parts = [np.where(np.arange(16) < 11, np.arange(16), 10**6)]
        for side in (near, -near):
            parts.append(np.where(np.arange(16) < 11, np.arange(16) + (8 if side > 0 else -8), 10**6))
        for side in (far, -far):
            parts.append(np.where(np.arange(8) < 3, np.arange(8) + (16 if side > 0 else -8), 10**6))
        coarse = coarse_kernel(np.arange(16)[:, None] - np.concatenate(parts)[None, :].astype(np.float64))
        coarse[11:] = 0
        fines.append(fine)
        coarses.append(coarse)
    down = hat(np.arange(24)[None, :] - (2.0 * np.arange(16)[:, None] - 1))
    down[11:] = 0
    up = hat(np.arange(24)[:, None] - (2.0 * np.arange(16)[None, :] - 1))
    up[19:] = 0
    up[:, 11:] = 0
    stack = lambda m: np.concatenate([halves(m)[0], halves(m)[1], halves(m)[0]], 1)
    thrice = lambda m: np.concatenate([halves(m)[0]] * 3, 1)
    return np.stack([stack(m) for m in fines]), np.stack([stack(m) for m in coarses]), thrice(down), thrice(up)


def z_prolong():
    result = np.zeros((128, 256))
    point = 2.0 * np.arange(67) - 1
    result[8:75, :131] = hat(np.arange(131)[None, :] - point[:, None])
    return halves(result)[0]


def split2(value):
    high = value.astype(bf16)
    return high, (value - high.astype(f32)).astype(bf16)


def split3(value):
    high = value.astype(bf16).astype(f32)
    rest = value - high
    middle = rest.astype(bf16).astype(f32)
    return high, middle, rest - middle


def dot(left, right):
    return jnp.dot(left, right, preferred_element_type=f32)


def spline(shifted):
    magnitude = jnp.abs(shifted)
    margin = jnp.maximum(1.5 - magnitude, 0.0)
    return jnp.where(magnitude < 0.5, 0.75 - shifted * shifted, 0.5 * margin * margin)


def spline_slope(shifted):
    magnitude = jnp.abs(shifted)
    margin = jnp.maximum(1.5 - magnitude, 0.0)
    return jnp.where(magnitude < 0.5, -2.0 * shifted, jnp.where(shifted > 0.0, -margin, margin))


def weights_at(offset, rows, first):
    points = lax.broadcasted_iota(i32, (rows, 128), 0).astype(f32)
    return 8.0 * offset + (1.0 + first) - points


def inside_mask(shape, dim, start, count):
    point = lax.broadcasted_iota(i32, shape, dim) + start
    return ((point >= 0) & (point < count)).astype(f32)


def spread_kernel(off_ref, charge_ref, counts_ref, near_ref, rho_ref, msg_ref):
    dx, dy, dz = lax.axis_index("gx"), lax.axis_index("gy"), lax.axis_index("ga")
    lane = lax.broadcasted_iota(i32, (1, 128), 1)
    row8 = lax.broadcasted_iota(i32, (8, 128), 0)
    rho_ref[...] = jnp.zeros((19, 24, 256), f32)
    zero8 = jnp.zeros((8, 128), f32)
    for i in range(2):
        for j in range(2):
            near_ref[i, j, 0] = zero8
            near_ref[i, j, 17] = zero8

    def column(ij, _):
        i, j = ij >> 1, ij & 1
        shift_x = 8.0 * (i + 1).astype(f32)
        shift_y = 8.0 * (j + 1).astype(f32)
        total = jnp.zeros((176, 128), f32)
        tail = None
        for m in range(8):
            highs, lows, z_highs, z_lows = [], [], [], []
            for half in range(2):
                k = 2 * m + half
                ox = off_ref[0, i, j, k : k + 1]
                oy = off_ref[1, i, j, k : k + 1]
                oz = off_ref[2, i, j, k : k + 1]
                count = counts_ref[i, j, k]
                weighted = jnp.where(lane < count, charge_ref[i, j, k : k + 1], 0.0)
                near_ref[i, j, k + 1] = jnp.concatenate(
                    [8.0 * ox + shift_x, 8.0 * oy + shift_y, 8.0 * oz + 8.0 * (k + 1), weighted, zero8[:4]], 0
                )
                wx = spline(weights_at(ox, 16, 0)) * weighted
                wy = spline(weights_at(oy, 16, 0))
                wz = spline(weights_at(oz, 32, 8 * half))
                plane = jnp.concatenate([wx[a : a + 1] * wy for a in range(11)], 0)
                high, low = split2(plane)
                highs.append(high)
                lows.append(low)
                z_high, z_low = split2(wz)
                z_highs.append(z_high)
                z_lows.append(z_low)
            left = jnp.concatenate(highs + lows + highs, 1)
            right = jnp.concatenate(z_highs + z_highs + z_lows, 1)
            if m < 7:
                pieces = [right]
                if m > 0:
                    pieces = [jnp.zeros((16 * m, 768), bf16)] + pieces
                if m < 6:
                    pieces = pieces + [jnp.zeros((96 - 16 * m, 768), bf16)]
                total = total + lax.dot_general(left, jnp.concatenate(pieces, 0), LAST, preferred_element_type=f32)
            else:
                wide = jnp.concatenate([jnp.zeros((112, 768), bf16), right, jnp.zeros((112, 768), bf16)], 0)
                both = lax.dot_general(left, wide, LAST, preferred_element_type=f32)
                total = total + both[:, :128]
                tail = both[:, 128:]
        first = pl.multiple_of(8 * j, 8)
        for a in range(11):
            rho_ref[8 * i + a, pl.ds(first, 16), 0:128] += total[16 * a : 16 * a + 16]
            rho_ref[8 * i + a, pl.ds(first, 16), 128:256] += tail[16 * a : 16 * a + 16]
        return 0

    lax.fori_loop(0, 4, column, 0)
    mask_y = inside_mask((24, 256), 0, 16 * dy - 1, 128)
    mask_z = inside_mask((24, 256), 1, 128 * dz - 1, 256)
    mask = mask_y * mask_z
    wide_lane = lax.broadcasted_iota(i32, (24, 128), 1)
    lane8 = lax.broadcasted_iota(i32, (8, 128), 1)
    block = jnp.zeros((8, 128), i32)
    for n in range(64):
        block = jnp.where(lane8 == n, counts_ref[n >> 5, (n >> 4) & 1, n & 15], block)
    msg_ref[0:8] = block.astype(f32)
    for i in range(2):
        picked = [jnp.where(dz == 0, near_ref[i, j, 16], near_ref[i, j, 1]) for j in range(2)]
        msg_ref[8 + 8 * i : 16 + 8 * i] = jnp.where(row8 < 4, picked[0], pltpu.roll(picked[1], 4, 0))
    faces = []
    for a in range(19):
        point = 16 * dx - 1 + a
        keep = ((point >= 0) & (point < 128)).astype(f32)
        plane = rho_ref[a] * (mask * keep)
        rho_ref[a] = plane
        low, high = plane[:, :128], plane[:, 128:]
        top = jnp.where(wide_lane < 18, pltpu.roll(low, 18, 1), pltpu.roll(high, 18, 1))
        face = jnp.where(dz == 0, top, low)
        faces.append(jnp.where(wide_lane < 21, face, 0.0))
    faces.append(jnp.zeros((24, 128), f32))
    for p in range(5):
        packed = faces[p]
        for g in range(1, 4):
            packed = packed + pltpu.roll(faces[5 * g + p], 32 * g, 1)
        msg_ref[24 + 24 * p : 48 + 24 * p] = packed


def along_z_kernel(near_ref, rho_ref, own_msg_ref, got_ref, op_ref, down_ref,
                   near1_ref, full_ref, restr_ref, a_ref, b_ref, m_ref, n_ref):
    dy, dz = lax.axis_index("gy"), lax.axis_index("ga")
    even, far = (dy & 1) == 0, (dy & 2) == 0
    row8 = lax.broadcasted_iota(i32, (8, 128), 0)
    shift = jnp.where(row8 == 2, jnp.where(dz == 0, 128.0, -128.0), 0.0)
    for i in range(2):
        got = got_ref[8 + 8 * i : 16 + 8 * i]
        parts = [jnp.where(row8 < 4, got, 0.0), jnp.where(row8 < 4, pltpu.roll(got, 4, 0), 0.0)]
        for j in range(2):
            near1_ref[i, j, 1:17] = near_ref[i, j, 1:17]
            moved = parts[j] + shift
            near1_ref[i, j, 0] = jnp.where(dz == 1, moved, 0.0)
            near1_ref[i, j, 17] = jnp.where(dz == 0, moved, 0.0)
    lane = lax.broadcasted_iota(i32, (24, 128), 1)
    high_op, low_op = op_ref[dz, 0], op_ref[dz, 1]
    down = down_ref[...]
    lane16 = lax.broadcasted_iota(i32, (16, 128), 1)
    keep = inside_mask((16, 128), 0, 8 * dy - 1, 64)
    for g in range(4):
        planes = range(5 * g, min(5 * g + 5, 19))
        stacked = []
        for p, a in enumerate(planes):
            face = pltpu.roll(got_ref[24 + 24 * p : 48 + 24 * p], (32 - 32 * g) % 128, 1)
            second = jnp.where((lane >= 32) & (lane < 64), face, rho_ref[a, :, 128:256])
            stacked.append(jnp.concatenate([rho_ref[a, :, 0:128], second], 1))
        high, low = split2(jnp.concatenate(stacked, 0))
        result = dot(high, high_op) + dot(low, high_op) + dot(high, low_op)
        for p, a in enumerate(planes):
            plane = result[24 * p : 24 * p + 24]
            full_ref[a] = plane
            h, m, l = split3(plane[:, 128:256])
            restricted = dot(down, jnp.concatenate([h, m, l], 0).astype(bf16)) * keep
            restr_ref[a] = restricted
            for out, way in ((a_ref, even), (b_ref, ~even)):
                window = jnp.where(way, plane[8:24], plane[0:16])
                out[152 + 16 * a : 168 + 16 * a] = window[:, 0:128]
                out[456 + 16 * a : 472 + 16 * a] = jnp.where(lane16 < 8, window[:, 128:256], restricted)
            m_ref[8 * a : 8 * a + 8] = jnp.where(far, restricted[8:16], restricted[0:8])
            n_ref[8 * a : 8 * a + 8] = jnp.where(far, restricted[0:8], restricted[8:16])
    counts = jnp.where(row8 == 0, own_msg_ref[0:8], jnp.where(row8 == 1, pltpu.roll(got_ref[0:8], 1, 0), 0.0))
    for out, j in ((a_ref, 1 - (dy & 1)), (b_ref, dy & 1)):
        out[0:8] = counts
        for level in range(18):
            out[8 + 8 * level : 16 + 8 * level] = jnp.where(
                row8 < 4, near1_ref[0, j, level], pltpu.roll(near1_ref[1, j, level], 4, 0)
            )


def along_y_kernel(near1_ref, full_ref, restr_ref, own_msg_ref, got_a_ref, got_b_ref, got_m_ref, got_n_ref,
                   fine_ref, coarse_ref, after_ref, near2_ref, fine2_ref, coarse2_ref,
                   a_ref, b_ref, m_ref, n_ref):
    dx, dy = lax.axis_index("gx"), lax.axis_index("gy")
    even, odd_x = (dy & 1) == 0, dx & 1
    far_x = (dx & 2) == 0
    row8 = lax.broadcasted_iota(i32, (8, 128), 0)
    keep = inside_mask((16, 128), 0, 8 * dy - 1, 64)
    lane16 = lax.broadcasted_iota(i32, (16, 128), 1)
    lane24 = lax.broadcasted_iota(i32, (24, 128), 1)
    fine_op, coarse_op = fine_ref[dy & 3], coarse_ref[dy & 3]

    def plane(a, _):
        at = pl.multiple_of(16 * a, 16)
        at8 = pl.multiple_of(8 * a, 8)
        a_low, a_high = got_a_ref[pl.ds(152 + at, 16)], got_a_ref[pl.ds(456 + at, 16)]
        b_low, b_high = got_b_ref[pl.ds(152 + at, 16)], got_b_ref[pl.ds(456 + at, 16)]
        stack = jnp.concatenate(
            [full_ref[a], jnp.concatenate([a_low, a_high], 1), jnp.concatenate([b_low, b_high], 1)], 0
        )
        high, low = split3(stack)[:2]
        fine2_ref[a] = dot(fine_op, jnp.concatenate([high, high, low], 0).astype(bf16))
        stack = jnp.concatenate(
            [restr_ref[a], a_high, b_high, got_m_ref[pl.ds(at8, 8)], got_n_ref[pl.ds(at8, 8)]], 0
        )
        high, low = split3(stack)[:2]
        coarse2_ref[a] = dot(coarse_op, jnp.concatenate([high, high, low], 0).astype(bf16)) * keep
        return 0

    lax.fori_loop(0, 19, plane, 0)
    restricted = []
    for e in range(11):
        value = None
        for a, weight in ((2 * e - 2, 0.5), (2 * e - 1, 1.0), (2 * e, 0.5)):
            if 0 <= a < 19:
                term = coarse2_ref[a] * weight
                value = term if value is None else value + term
        point = 8 * dx - 1 + e
        restricted.append(value * ((point >= 0) & (point < 64)).astype(f32))
    blank = jnp.zeros((8, 128), f32)
    for out, first in ((a_ref, 8 * (1 - odd_x)), (b_ref, 8 * odd_x)):
        for n in range(11):
            plane_value = fine2_ref[first + n]
            out[296 + 24 * n : 320 + 24 * n] = plane_value[:, 0:128]
            out[560 + 24 * n : 584 + 24 * n] = jnp.where(
                lane24 < 8, plane_value[:, 128:256], jnp.concatenate([restricted[n], blank], 0)
            )
    for n in range(3):
        m_ref[16 * n : 16 * n + 16] = jnp.where(far_x, restricted[8 + n], restricted[n])
        n_ref[16 * n : 16 * n + 16] = jnp.where(far_x, restricted[n], restricted[8 + n])
    shift_a = jnp.where(row8 == 1, jnp.where(even, 16.0, -16.0), 0.0)
    at_a = 3 * (1 - (dy & 1))
    for level in range(18):
        for y, source, shift in ((at_a, got_a_ref, shift_a), (3 - at_a, got_b_ref, -shift_a)):
            got = source[8 + 8 * level : 16 + 8 * level]
            near2_ref[0, y, level] = jnp.where(row8 < 4, got, 0.0) + shift
            near2_ref[1, y, level] = jnp.where(row8 < 4, pltpu.roll(got, 4, 0), 0.0) + shift
        for x in range(2):
            for y in range(2):
                near2_ref[x, y + 1, level] = near1_ref[x, y, level]
    below, above = jnp.where(even, got_b_ref[0:8], got_a_ref[0:8]), jnp.where(even, got_a_ref[0:8], got_b_ref[0:8])
    counts = jnp.where(row8 < 2, own_msg_ref[0:8], 0.0)
    counts = jnp.where((row8 >= 2) & (row8 < 4), pltpu.roll(below, 2, 0), counts)
    counts = jnp.where((row8 >= 4) & (row8 < 6), pltpu.roll(above, 4, 0), counts)
    for out, x in ((a_ref, 1 - odd_x), (b_ref, odd_x)):
        out[0:8] = counts
        for level in range(18):
            for pair in range(2):
                at = 8 + 8 * (2 * level + pair)
                out[at : at + 8] = jnp.where(
                    row8 < 4, near2_ref[x, 2 * pair, level], pltpu.roll(near2_ref[x, 2 * pair + 1, level], 4, 0)
                )


def along_x_kernel(fine2_ref, own_msg_ref, got_a_ref, got_b_ref, got_m_ref, got_n_ref,
                   up_y_ref, up_z_ref, after_ref, phi_ref, source, third, coarse):
    dx, dy, dz = lax.axis_index("gx"), lax.axis_index("gy"), lax.axis_index("ga")
    even, far = 1 - (dx & 1), 1 - ((dx >> 1) & 1)
    for p in range(8):
        source[p] = jnp.zeros((24, 256), f32)
        source[27 + p] = jnp.zeros((24, 256), f32)
        coarse[p] = jnp.zeros((16, 128), f32)
        coarse[19 + p] = jnp.zeros((16, 128), f32)
    for p in range(19):
        source[8 + p] = fine2_ref[p]
    for got, first in ((got_a_ref, 24 * even), (got_b_ref, 24 * (1 - even))):
        for n in range(11):
            source[first + n, :, 0:128] += got[296 + 24 * n : 320 + 24 * n]
            source[first + n, :, 128:256] += got[560 + 24 * n : 584 + 24 * n]
    for n in range(11):
        coarse[8 + n] = own_msg_ref[560 + 24 * n : 576 + 24 * n]
    for got, first in ((got_a_ref, 16 * even), (got_b_ref, 16 * (1 - even))):
        for n in range(11):
            coarse[first + n] += got[560 + 24 * n : 576 + 24 * n]
    for got, first in ((got_m_ref, 24 * far), (got_n_ref, 24 * (1 - far))):
        for n in range(3):
            coarse[first + n] += got[16 * n : 16 * n + 16]
    fine_weights = [float(w) for w in fine_kernel(np.arange(9.0))]
    coarse_weights = [float(w) for w in coarse_kernel(np.arange(9.0))]

    def fine_plane(a, _):
        value = source[a + 8] * (4.0 * fine_weights[0])
        for d in range(1, 9):
            value = value + (source[a + 8 - d] + source[a + 8 + d]) * (4.0 * fine_weights[d])
        third[a] = value
        return 0

    lax.fori_loop(0, 19, fine_plane, 0)

    lifted = []
    up_y, up_z = up_y_ref[...], up_z_ref[...]
    for e in range(11):
        value = coarse[e + 8] * (2.0 * coarse_weights[0])
        for d in range(1, 9):
            value = value + (coarse[e + 8 - d] + coarse[e + 8 + d]) * (2.0 * coarse_weights[d])
        point = 8 * dx - 1 + e
        value = value * ((point >= 0) & (point < 64)).astype(f32)
        h, m, l = split3(value)
        tall = dot(up_y, jnp.concatenate([h, m, l], 0).astype(bf16))
        h, m, l = split3(tall)
        stacked = jnp.concatenate([h, m, l], 0).astype(bf16)
        wide = dot(stacked, up_z)
        lifted.append(wide[0:24] + wide[24:48] + wide[48:72])
    mask = inside_mask((24, 256), 0, 16 * dy - 1, 128) * inside_mask((24, 256), 1, 128 * dz - 1, 256)
    lane = lax.broadcasted_iota(i32, (24, 256), 1)
    mask = jnp.where(lane < 131, mask, 0.0)
    for a in range(19):
        if a % 2:
            value = lifted[(a + 1) // 2]
        else:
            value = 0.5 * (lifted[a // 2] + lifted[a // 2 + 1])
        point = 16 * dx - 1 + a
        keep = mask * ((point >= 0) & (point < 128)).astype(f32)
        phi_ref[a] = jnp.where(keep > 0.0, third[a] + value, 0.0)


def gather_kernel(off_ref, charge_ref, counts_ref, phi_ref, out_ref):
    lane = lax.broadcasted_iota(i32, (1, 128), 1)
    lane176 = lax.broadcasted_iota(i32, (176, 128), 1)

    def column(ij, _):
        i, j = ij >> 1, ij & 1
        first = pl.multiple_of(8 * j, 8)
        low = jnp.concatenate([phi_ref[8 * i + a, pl.ds(first, 16), 0:128] for a in range(11)], 0)
        high = jnp.concatenate([phi_ref[8 * i + a, pl.ds(first, 16), 128:256] for a in range(11)], 0)
        for m in range(8):
            window = pltpu.roll(low, (128 - 16 * m) % 128, 1) if m else low
            if m == 7:
                window = jnp.where(lane176 < 16, window, pltpu.roll(high, 16, 1))
            window = jnp.where(lane176 < 32, window, 0.0)
            part_h = window.astype(bf16).astype(f32)
            part_m = window - part_h
            left = (part_h + pltpu.roll(part_m, 32, 1) + pltpu.roll(part_h, 64, 1)).astype(bf16)
            stacks, slopes, sides = [], [], []
            for half in range(2):
                k = 2 * m + half
                ox = off_ref[0, i, j, k : k + 1]
                oy = off_ref[1, i, j, k : k + 1]
                oz = off_ref[2, i, j, k : k + 1]
                count = counts_ref[i, j, k]
                weighted = jnp.where(lane < count, charge_ref[i, j, k : k + 1], 0.0)
                shifted = weights_at(oz, 32, 8 * half)
                for bag, value in ((stacks, spline(shifted)), (slopes, spline_slope(shifted))):
                    high_part, low_part = split2(value)
                    bag.append(jnp.concatenate([high_part, high_part, low_part, jnp.zeros((32, 128), bf16)], 0))
                sides.append((ox, oy, weighted))
            right = jnp.concatenate(stacks + slopes, 1)
            product = dot(left, right)
            for half in range(2):
                k = 2 * m + half
                ox, oy, weighted = sides[half]
                level = product[:, 128 * half : 128 * half + 128]
                rising = product[:, 256 + 128 * half : 384 + 128 * half]
                sx = weights_at(ox, 16, 0)
                sy = weights_at(oy, 16, 0)
                wx, gx = spline(sx), spline_slope(sx)
                wy, gy = spline(sy), spline_slope(sy)
                along = across = up = None
                for a in range(11):
                    piece = level[16 * a : 16 * a + 16]
                    rise = rising[16 * a : 16 * a + 16]
                    terms = (gx[a : a + 1] * piece, wx[a : a + 1] * piece, wx[a : a + 1] * rise)
                    if a == 0:
                        along, across, up = terms
                    else:
                        along, across, up = along + terms[0], across + terms[1], up + terms[2]
                force_x = jnp.sum(along * wy, axis=0, keepdims=True)
                force_y = jnp.sum(across * gy, axis=0, keepdims=True)
                force_z = jnp.sum(up * wy, axis=0, keepdims=True)
                out_ref[0, i, j, k : k + 1] = -weighted * force_x
                out_ref[1, i, j, k : k + 1] = -weighted * force_y
                out_ref[2, i, j, k : k + 1] = -weighted * force_z
        return 0

    lax.fori_loop(0, 4, column, 0)


def pair_scratch(form, cells, tiles):
    rows, slots, share = form
    sets = cells // share
    return (
        [
            pltpu.VMEM((tiles, 8, 128), f32),
            pltpu.VMEM((tiles, 48, 128), bf16),
            pltpu.VMEM((tiles, 16, 128), bf16),
            pltpu.VMEM((sets + 1, share * 128, 128), f32),
            pltpu.VMEM(((sets + 1) * (share * 128 // rows), 16, 128), f32),
        ]
        + [
            pltpu.VMEM((rows, TILES * 128), f32),
            pltpu.VMEM((rows, TILES * 128), bf16),
            pltpu.VMEM((rows, TILES * 128), bf16),
        ]
        * slots
        + [pltpu.SMEM((128,), i32), pltpu.SMEM((cells,), i32)]
        + [pltpu.SMEM((sets + 1,), i32)] * 3
    )


def middle_of(center):
    row = lax.broadcasted_iota(i32, (8, 128), 0)
    return jnp.where(row < 2, 16.0, jnp.where(row == 2, center, 0.0))


def pack_list(packed, start, base, tile, levels, center):
    lane = lax.broadcasted_iota(i32, (8, 128), 1)
    middle = middle_of(center)
    end, current = tile * 128, jnp.zeros((8, 128), f32)
    for level, beads in enumerate(levels):
        start[base + level] = end
        for value, count in beads:
            within, tile = end & 127, end >> 7
            turned = pltpu.roll(value - middle, within, 1)
            keep = lane < within
            current = jnp.where(keep, current, turned)
            packed[tile] = current
            end = end + count
            current = jnp.where((end >> 7) > tile, jnp.where(keep, turned, 0.0), current)
    start[base + 10] = end
    packed[end >> 7] = jnp.where(lane < (end & 127), current, 0.0)
    for e in range(1, TILES):
        packed[(end >> 7) + e] = jnp.zeros((8, 128), f32)
    return (end >> 7) + TILES


def pair_sums(scratch, form, cells, used, own_pos, own_count, own_start, own_center, emit):
    packed, features, sources, own_features, sums = scratch[:5]
    start, row_at, first_tile, groups_of, blocks_of = scratch[-5:]
    height, flight, share = form
    sets = cells // share
    slots = [scratch[5 + 3 * e : 8 + 3 * e] for e in range(flight)]
    blocks = share * 128 // height
    lane = lax.broadcasted_iota(i32, (16, 128), 1)
    row = lax.broadcasted_iota(i32, (8, 128), 0)
    for e in range(8):
        packed[used + e] = jnp.zeros((8, 128), f32)

    def near_step(step, _):
        for e in range(8):
            tile = 8 * step + e
            value = packed[tile]
            norm = value[0:1] * value[0:1] + value[1:2] * value[1:2] + value[2:3] * value[2:3]
            vector = jnp.where(row < 3, value, jnp.where(row == 3, norm, jnp.where(row == 4, 1.0, 0.0)))
            h, m, l = split3(vector)
            features[tile] = jnp.concatenate([h, h, m, m, h, l], 0).astype(bf16)
            charge = value[3:4]
            vector = jnp.where(row < 3, value * charge, jnp.where(row == 3, charge, 0.0))
            h, m, l = split3(vector)
            sources[tile] = jnp.concatenate(
                [jnp.where(row < 4, h, pltpu.roll(m, 4, 0)), jnp.where(row < 4, l, 0.0)], 0
            ).astype(bf16)
        return 0

    lax.fori_loop(0, (used + 7) // 8, near_step, 0)

    def own_one(n, which, at):
        value = own_pos(n) - middle_of(own_center(n))
        norm = value[0:1] * value[0:1] + value[1:2] * value[1:2] + value[2:3] * value[2:3]
        vector = jnp.where(
            row < 3,
            value * (2.0 / 64),
            jnp.where(row == 3, -1.0 / 64, jnp.where(row == 4, 1.0 - norm * (1.0 / 64), 0.0)),
        )
        h, m, l = split3(vector)
        stacked = jnp.concatenate([h, m, h, m, l, h, jnp.zeros((80, 128), f32)], 0)
        own_features[which, pl.ds(pl.multiple_of(at, 8), 128), :] = jnp.transpose(stacked)
        row_at[n] = at
        return at + ((own_count(n) + 7) >> 3) * 8

    def own_step(step, total):
        for e in range(8 // share):
            which = step * (8 // share) + e
            at = i32(0)
            for c in range(share):
                at = own_one(c * sets + which, which, at)
            for b in range(blocks):
                sums[which * blocks + b] = jnp.zeros((16, 128), f32)
            level = own_start(which)
            begin, stop = start[level], start[level + 3]
            tile = begin >> 7
            groups = jnp.maximum((((stop + 127) >> 7) - tile + TILES - 1) // TILES, 1)
            rows = (at + height - 1) // height
            first_tile[which], groups_of[which], blocks_of[which] = tile, groups, rows
            total = total + groups * rows
        return total

    total = lax.fori_loop(0, cells // 8, own_step, i32(0))
    own_features[sets] = jnp.zeros((share * 128, 128), f32)
    for e in range(blocks):
        sums[sets * blocks + e] = jnp.zeros((16, 128), f32)
    first_tile[sets], groups_of[sets], blocks_of[sets] = i32(0), i32(1), i32(1)
    for distance, high, low in slots:
        distance[...] = jnp.zeros((height, TILES * 128), f32)
        high[...] = jnp.zeros((height, TILES * 128), bf16)
        low[...] = jnp.zeros((height, TILES * 128), bf16)

    def item(_, state):
        cell, block, group = state[:3]
        older, oldest = state[3 : 3 + 2 * flight], state[3 + 2 * flight :]
        added, shares, fresh, tags = [], [], [], []
        for e in range(flight):
            distance, high, low = slots[e]
            tile = oldest[2 * e + 1]
            source = jnp.concatenate([sources[tile + s] for s in range(TILES)], 1)
            added.append(
                lax.dot_general(
                    jnp.concatenate([source, source], 1),
                    jnp.concatenate([high[...], low[...]], 1),
                    LAST,
                    preferred_element_type=f32,
                )
            )
            reach = distance[...]
            kept = jnp.maximum(reach, 0.0)
            strength = (kept * kept * kept) / (CAP - reach)
            shares.append(split2(strength))
            groups, rows = groups_of[cell], blocks_of[cell]
            tile = first_tile[cell] + group * TILES
            at = pl.multiple_of(block * height, height)
            left = own_features[cell, pl.ds(at, height), 0:48].astype(bf16)
            right = jnp.concatenate([features[tile + s] for s in range(TILES)], 1)
            fresh.append(dot(left, right))
            tags += [cell * blocks + block, tile]
            group = group + 1
            wrap = (group >= groups).astype(i32)
            group = group * (1 - wrap)
            block = block + wrap
            wrap = (block >= rows).astype(i32)
            block = block * (1 - wrap)
            cell = jnp.minimum(cell + wrap, sets)
        for e in range(flight):
            distance, high, low = slots[e]
            where = oldest[2 * e]
            sums[where, :, 0:height] = sums[where, :, 0:height] + added[e]
            high[...], low[...] = shares[e]
            distance[...] = fresh[e]
        return (cell, block, group) + tuple(tags) + tuple(older)

    spare = (i32(sets * blocks), i32(0))
    lax.fori_loop(0, (total + flight - 1) // flight + 2, item, (i32(0),) * 3 + spare * (2 * flight))

    def finish_one(n):
        if share == 1:
            parts = [sums[n * blocks + e, :, 0:height] for e in range(blocks)]
            whole = jnp.concatenate(parts, 1) if blocks > 1 else parts[0]
        else:
            at = row_at[n]
            block, within = (n % sets) * blocks + (at >> 7), at & 127
            back = (128 - within) & 127
            whole = jnp.where(
                lane < 128 - within, pltpu.roll(sums[block], back, 1), pltpu.roll(sums[block + 1], back, 1)
            )
        whole = whole[0:4] + whole[4:8] + whole[8:12]
        raw = own_pos(n)
        value = raw - middle_of(own_center(n))
        emit(n, (value[0:3] * whole[3:4] - whole[0:3]) * (raw[3:4] * (1.0 / 64)), raw)

    def finish(step, _):
        for e in range(4):
            finish_one(4 * step + e)
        return 0

    lax.fori_loop(0, cells // 4, finish, 0)


def inner_pairs_kernel(part, near_ref, counts_ref, partners_ref, after_ref, out_ref, table, *scratch):
    lane = lax.broadcasted_iota(i32, (1, 128), 1)
    for column in range(4):
        table[18 * column] = i32(0)
        table[18 * column + 17] = i32(0)

    def copy_count(k, _):
        for column in range(4):
            table[18 * column + 1 + k] = counts_ref[column >> 1, column & 1, k]
        return 0

    lax.fori_loop(0, 16, copy_count, 0)

    levels = [[(near_ref[18 * c + 8 * part + n], table[18 * c + 8 * part + n]) for c in range(4)] for n in range(10)]
    used = pack_list(scratch[0], scratch[-5], 0, i32(0), levels, 64.0 * part + 40.0)

    def cell_at(n):
        return (n >> 3) * 18 + (n & 7) + (8 * part + 1)

    def emit(n, value, raw):
        x, y, k = n >> 4, (n >> 3) & 1, 8 * part + (n & 7)
        count = table[cell_at(n)]
        partner = partners_ref[x, y, pl.ds(k, 1), :]
        other = jnp.take_along_axis(raw, jnp.broadcast_to(partner, (8, 128)), axis=1)
        both = (lane < count) & (partner < count)
        out_ref[x, y, n & 7, 0:3] = value + jnp.where(both, -0.1 * (raw[0:3] - other[0:3]), 0.0)

    pair_sums(
        scratch,
        INNER,
        32,
        used,
        lambda n: near_ref[cell_at(n)],
        lambda n: table[cell_at(n)],
        lambda n: n & 7,
        lambda n: 64.0 * part + 40.0,
        emit,
    )


def outer_pairs_kernel(near2_ref, own_msg_ref, got_a_ref, got_b_ref, first_ref, second_ref, out_ref,
                       near, counts, table, *scratch):
    dz, odd = lax.axis_index("ga"), lax.axis_index("gx") & 1
    row8 = lax.broadcasted_iota(i32, (8, 128), 0)
    for n, source in enumerate((got_a_ref, own_msg_ref, got_b_ref)):
        pltpu.sync_copy(source.at[0:8], counts.at[n])
    shift_a = jnp.where(row8 == 0, jnp.where(odd == 0, 16.0, -16.0), 0.0)
    at_a = 3 * (1 - odd)

    def level_step(level, _):
        for x in range(2):
            for y in range(4):
                near[(4 * x + 4 + y) * 18 + level] = near2_ref[x, y, level]
        for x, source, shift in ((at_a, got_a_ref, shift_a), (3 - at_a, got_b_ref, -shift_a)):
            for pair in range(2):
                at = pl.multiple_of(8 + 8 * (2 * level + pair), 8)
                got = source[pl.ds(at, 8)]
                near[(4 * x + 2 * pair) * 18 + level] = jnp.where(row8 < 4, got, 0.0) + shift
                near[(4 * x + 2 * pair + 1) * 18 + level] = jnp.where(row8 < 4, pltpu.roll(got, 4, 0), 0.0) + shift
        return 0

    lax.fori_loop(0, 18, level_step, 0)
    for x in range(4):
        which, along = ((2 * (1 - odd), 1), (1, 0), (1, 1), (2 * odd, 0))[x]
        for y in range(4):
            pair_row, across = ((2, 1), (0, 0), (0, 1), (4, 0))[y]
            base = 32 * along + 16 * across
            at = (x * 4 + y) * 18
            table[at] = jnp.where(dz == 1, counts[which, pair_row + 1, base + 15], 0.0).astype(i32)
            table[at + 17] = jnp.where(dz == 0, counts[which, pair_row + 1, base], 0.0).astype(i32)

            def copy_count(k, _, which=which, pair_row=pair_row, base=base, at=at):
                table[at + 1 + k] = counts[which, pair_row, base + k].astype(i32)
                return 0

            lax.fori_loop(0, 16, copy_count, 0)

    def split(number):
        return number >> 2, (number >> 1) & 1, number & 1

    def one_list(number, tile):
        i, j, part = split(number)
        outside = [(12 * i + j + c) * 18 + 8 * part for c in range(3)]
        outside += [(4 * x + 3 * j) * 18 + 8 * part for x in (1, 2)]
        within = [(4 * x + y) * 18 + 8 * part for x in (1, 2) for y in (1, 2)]
        levels = []
        for level in range(10):
            beads = [(near[base + level], table[base + level]) for base in outside]
            if level in (0, 9):
                use = part if level else 1 - part
                beads += [(near[base + level], table[base + level] * use) for base in within]
            levels.append(beads)
        return pack_list(scratch[0], scratch[-5], 16 * number, tile, levels, 64.0 * part.astype(f32) + 40.0)

    used = lax.fori_loop(0, 8, one_list, i32(0))

    def own_at(n):
        i, j, part = split(n >> 3)
        return (4 * (i + 1) + j + 1) * 18 + 8 * part + 1 + (n & 7)

    def emit(n, value, raw):
        i, j, part = split(n >> 3)
        value = value + jnp.where(part == 0, first_ref[i, j, n & 7, 0:3], second_ref[i, j, n & 7, 0:3])
        for d in range(3):
            out_ref[d, i, j, pl.ds(8 * part + (n & 7), 1), :] = value[d : d + 1]

    pair_sums(
        scratch,
        OUTER,
        64,
        used,
        lambda n: near[own_at(n)],
        lambda n: table[own_at(n)],
        lambda n: 16 * (n >> 3) + (n & 7),
        lambda n: 64.0 * ((n >> 3) & 1).astype(f32) + 40.0,
        emit,
    )


def call(kernel, shapes, inputs, specs=None, scratch=(), flops=10**6, out_specs=None):
    single = not isinstance(shapes, (list, tuple)) or isinstance(shapes[0], int)
    shapes = [shapes] if single else shapes
    result = pl.pallas_call(
        kernel,
        out_shape=[jax.ShapeDtypeStruct(s, f32) for s in shapes],
        in_specs=specs or [VMEM] * len(inputs),
        out_specs=[VMEM] * len(shapes),
        scratch_shapes=list(scratch),
        cost_estimate=pl.CostEstimate(flops=flops, transcendentals=0, bytes_accessed=10**6),
        compiler_params=pltpu.CompilerParams(vmem_limit_bytes=40 << 20),
    )(*inputs)
    return result[0] if single else result


PARTNERS = (
    ((0, 1), (2, 3), (4, 5), (6, 7)),
    ((1, 2), (3, 4), (5, 6)),
    ((0, 2), (1, 3), (4, 6), (5, 7)),
    ((2, 4), (3, 5)),
)


def exchange(messages, axis):
    return [
        lax.ppermute(value, axis, [way for p, q in pairs for way in ((p, q), (q, p))])
        for value, pairs in zip(messages, PARTNERS)
    ]


def per_device(offsets, charge, counts, partners):
    z_op = jnp.asarray(np.stack([np.stack(halves(z_operator(part))) for part in range(2)]))
    fine_op, coarse_op, y_down, y_up = [jnp.asarray(m) for m in y_operators()]
    z_up = jnp.asarray(z_prolong())
    near, rho, z_msg = call(
        spread_kernel,
        [(2, 2, 18, 8, 128), (19, 24, 256), (144, 128)],
        (offsets, charge, counts),
        [VMEM, VMEM, SMEM],
    )
    z_got = lax.ppermute(z_msg, "ga", [(0, 1), (1, 0)])
    near1, full, restr, *y_msgs = call(
        along_z_kernel,
        [(2, 2, 18, 8, 128), (19, 24, 256), (19, 16, 128), (760, 128), (760, 128), (152, 128), (152, 128)],
        (near, rho, z_msg, z_got, z_op, y_down),
    )
    y_got = exchange(y_msgs, "gy")
    inner = lambda part, near_in, after: call(
        lambda *refs: inner_pairs_kernel(part, *refs),
        (2, 2, 8, 8, 128),
        (near_in.reshape(72, 8, 128), counts, partners, after),
        [VMEM, SMEM, VMEM, ANY],
        [pltpu.SMEM((72,), i32)] + pair_scratch(INNER, 32, 40 + TILES + 16),
        flops=10**9,
    )
    first = inner(0, near, full)
    near2, fine2, _, *x_msgs = call(
        along_y_kernel,
        [(2, 4, 18, 8, 128), (19, 24, 256), (19, 16, 128), (824, 128), (824, 128), (48, 128), (48, 128)],
        (near1, full, restr, y_msgs[0], *y_got, fine_op, coarse_op, first),
        [VMEM] * 10 + [ANY],
    )
    x_got = exchange(x_msgs, "gx")
    second = inner(1, near, fine2)
    phi = call(
        along_x_kernel,
        (19, 24, 256),
        (fine2, x_msgs[0], *x_got, y_up, z_up, second),
        [VMEM] * 8 + [ANY],
        [pltpu.VMEM((35, 24, 256), f32), pltpu.VMEM((19, 24, 256), f32), pltpu.VMEM((27, 16, 128), f32)],
    )
    short_force = call(
        outer_pairs_kernel,
        (3, 2, 2, 16, 128),
        (near2, x_msgs[0], x_got[0], x_got[1], first, second),
        None,
        [
            pltpu.VMEM((288, 8, 128), f32),
            pltpu.SMEM((3, 8, 128), f32),
            pltpu.SMEM((288,), i32),
        ]
        + pair_scratch(OUTER, 64, 8 * (54 + TILES) + 24),
        flops=10**9,
    )
    long_force = call(
        gather_kernel, (3, 2, 2, 16, 128), (offsets, charge, counts, phi), [VMEM, VMEM, SMEM, VMEM]
    )
    return short_force, long_force


def solution(mesh):
    return jax.shard_map(
        per_device,
        mesh=mesh,
        in_specs=(
            P(None, "gx", "gy", "ga", None),
            P("gx", "gy", "ga", None),
            P("gx", "gy", "ga"),
            P("gx", "gy", "ga", None),
        ),
        out_specs=(P(None, "gx", "gy", "ga", None), P(None, "gx", "gy", "ga", None)),
        check_vma=False,
    )
```

profile of v0, /device:TPU:115, one launch (start us, length us, event | category | flops | bytes accessed | tf_op | source)
XLA Modules:
  0.0 94.1 jit_solution(5621196364688309589)
XLA Ops:
  0.6 0.9 copy-done.1
  1.5 0.8 copy-done.3
  2.3 0.7 copy-done.8
  3.0 4.1 %shard_map.113 = (f32[2,2,18,8,128]{4,3,2,1,0:T(8,128)S(1)}, f32[19,24,256]{2,1,0:T(8,128)S(1)}, f32[144,128]{1,0:T(8,128)S(1)}) custom-call(f32[3,2,2,16,128]{4,3,2,1,0:T(8,128)S(1)} %copy-done.1, f32[2,2,16,128]{3,2,1,0:T(8,128)S(1)} %copy-done.3, s32[2,2,16]{2,1,0:T(2,128)S(1)} %copy-done.8), custom_call_target="tpu_custom_call" | custom-call | flops 1000000 | bytes 1000000 | tf_op jit(solution)/shard_map/pallas_call | solution.py:774
  7.1 0.2 collective-permute-start
  7.3 3.1 %collective-permute-done.got_ref = f32[144,128]{1,0:T(8,128)S(1)} collective-permute-done((f32[144,128]{1,0:T(8,128)S(1)}, f32[144,128]{1,0:T(8,128)S(1)}, u32[]{:S(2)}, u32[]{:S(2)}) %collective-permute-start) | collective-permute-done | bytes 73760 | tf_op jit(solution)/shard_map/ppermute | solution.py:811
  10.4 1.0 %copy-done = bf16[2,2,256,256]{3,2,1,0:T(8,128)(2,1)S(1)} copy-done((bf16[2,2,256,256]{3,2,1,0:T(8,128)(2,1)S(1)}, bf16[2,2,256,256]{3,2,1,0:T(8,128)(2,1)}, u32[]{:S(2)}) %copy-start) | copy-done | bytes 524312
  11.5 1.1 %shard_map.114 = (f32[2,2,18,8,128]{4,3,2,1,0:T(8,128)S(1)}, f32[19,24,256]{2,1,0:T(8,128)S(1)}, f32[19,16,128]{2,1,0:T(8,128)S(1)}, f32[760,128]{1,0:T(8,128)S(...) custom-call(f32[2,2,18,8,128]{4,3,2,1,0:T(8,128)S(1)} %get-tuple-element.18.near_ref, ...), custom_call_target="tpu_custom_call" | custom-call | flops 1000000 | bytes 1000000 | tf_op jit(solution)/shard_map/pallas_call | solution.py:774
  12.6 3.1 %collective-permute-start.2 = (f32[760,128]{1,0:T(8,128)S(1)}, f32[760,128]{1,0:T(8,128)S(1)}, u32[]{:S(2)}, u32[]{:S(2)}) collective-permute-start(f32[760,128]{1,0:T(8,128)S(1)} %get-tuple-element.25), channel_id=1, source_target_pairs={{2,4},{4,2},{6,8},{8,6},{10,12},{12,10},{3,5},{5,3},{7,9},{9,7},{1... | collective-permute-start | bytes 1167368 | tf_op jit(solution)/shard_map/ppermute | solution.py:796
  15.7 1.8 %collective-permute-start.1 = (f32[760,128]{1,0:T(8,128)S(1)}, f32[760,128]{1,0:T(8,128)S(1)}, u32[]{:S(2)}, u32[]{:S(2)}) collective-permute-start(f32[760,128]{1,0:T(8,128)S(1)} %get-tuple-element.24.own_msg_ref), channel_id=1, source_target_pairs={{0,2},{2,0},{4,6},{6,4},{8,10},{10,8},{12,14},{14,12},{1,3},{3,1},... | collective-permute-start | bytes 1167368 | tf_op jit(solution)/shard_map/ppermute | solution.py:796
  17.5 4.4 %collective-permute-start.4 = (f32[152,128]{1,0:T(8,128)S(1)}, f32[152,128]{1,0:T(8,128)S(1)}, u32[]{:S(2)}, u32[]{:S(2)}) collective-permute-start(f32[152,128]{1,0:T(8,128)S(1)} %get-tuple-element.27), channel_id=1, source_target_pairs={{4,8},{8,4},{6,10},{10,6},{5,9},{9,5},{7,11},{11,7},{20,24},{24,20... | collective-permute-start | bytes 233480 | tf_op jit(solution)/shard_map/ppermute | solution.py:796
  22.0 0.0 copy-start.6
  22.0 0.0 copy-start.7
  22.0 8.8 %shard_map.115.after_ref.first_ref = f32[2,2,8,8,128]{4,3,2,1,0:T(8,128)S(1)} custom-call(f32[72,8,128]{2,1,0:T(8,128)S(1)} %bitcast.1, s32[2,2,16]{2,1,0:T(2,128)S(1)} %copy-done.9, s32[2,2,16,128]{3,2,1,0:T(8,128)S(1)} %copy-done.12, f32[19,24,256]{2,1,0:T(8,128)S(1)} %get-tuple-element.22.refs_3_.full_ref), custom_call_target="tpu_custom_call" | custom-call | flops 1000000000 | bytes 1000000 | tf_op jit(solution)/shard_map/pallas_call | solution.py:774
  30.8 5.3 %collective-permute-done.1.got_a_ref = f32[760,128]{1,0:T(8,128)S(1)} collective-permute-done((f32[760,128]{1,0:T(8,128)S(1)}, f32[760,128]{1,0:T(8,128)S(1)}, u32[]{:S(2)}, u32[]{:S(2)}) %collective-permute-start.1) | collective-permute-done | bytes 389152 | tf_op jit(solution)/shard_map/ppermute | solution.py:796
  36.1 3.6 %shard_map.116 = (f32[2,4,18,8,128]{4,3,2,1,0:T(8,128)S(1)}, f32[19,24,256]{2,1,0:T(8,128)S(1)}, f32[19,16,128]{2,1,0:T(8,128)}, f32[824,128]{1,0:T(8,128)S(1)},...) custom-call(f32[2,2,18,8,128]{4,3,2,1,0:T(8,128)S(1)} %get-tuple-element.21.near1_ref, ...), custom_call_target="tpu_custom_call" | custom-call | flops 1000000 | bytes 1000000 | tf_op jit(solution)/shard_map/pallas_call | solution.py:774
  39.8 3.3 %collective-permute-start.6 = (f32[824,128]{1,0:T(8,128)S(1)}, f32[824,128]{1,0:T(8,128)S(1)}, u32[]{:S(2)}, u32[]{:S(2)}) collective-permute-start(f32[824,128]{1,0:T(8,128)S(1)} %get-tuple-element.30), channel_id=1, source_target_pairs={{16,32},{32,16},{48,64},{64,48},{80,96},{96,80},{17,33},{33,17},{4... | collective-permute-start | bytes 1265672 | tf_op jit(solution)/shard_map/ppermute | solution.py:796
  43.0 0.1 collective-permute-start.5
  43.1 0.5 collective-permute-start.7
  43.6 2.1 %collective-permute-start.8 = (f32[48,128]{1,0:T(8,128)S(1)}, f32[48,128]{1,0:T(8,128)S(1)}, u32[]{:S(2)}, u32[]{:S(2)}) collective-permute-start(f32[48,128]{1,0:T(8,128)S(1)} %get-tuple-element.33), channel_id=1, source_target_pairs={{32,64},{64,32},{48,80},{80,48},{33,65},{65,33},{49,81},{81,49},{3... | collective-permute-start | bytes 73736 | tf_op jit(solution)/shard_map/ppermute | solution.py:796
  45.8 9.7 %shard_map.117.second_ref.after_ref = f32[2,2,8,8,128]{4,3,2,1,0:T(8,128)S(1)} custom-call(f32[72,8,128]{2,1,0:T(8,128)S(1)} %bitcast.2, s32[2,2,16]{2,1,0:T(2,128)S(1)} %copy-done.9, s32[2,2,16,128]{3,2,1,0:T(8,128)S(1)} %copy-done.12, f32[19,24,256]{2,1,0:T(8,128)S(1)} %get-tuple-element.31.refs_3_.fine2_ref), custom_call_target="tpu_custom_call" | custom-call | flops 1000000000 | bytes 1000000 | tf_op jit(solution)/shard_map/pallas_call | solution.py:774
  55.6 1.6 %shard_map.119.phi_ref = f32[19,24,256]{2,1,0:T(8,128)S(1)} custom-call(f32[19,24,256]{2,1,0:T(8,128)S(1)} %get-tuple-element.31.refs_3_.fine2_ref, f32[824,128]{1,0:T(8,128)S(1)} %get-tuple-element.29.own_msg_ref, f32[824,128]{1,0:T(8,128)S(1)} %collective-permute-done.5.got_a_ref, f32[824,128]{1,0:T(8,128)S(1)} %collective-permute-done.6.got_b_ref, ...), custom_call_target="tpu_custom_call" | custom-call | flops 1000000 | bytes 1000000 | tf_op jit(solution)/shard_map/pallas_call | solution.py:774
  57.2 6.0 %shard_map.120 = f32[3,2,2,16,128]{4,3,2,1,0:T(8,128)} custom-call(f32[3,2,2,16,128]{4,3,2,1,0:T(8,128)S(1)} %copy-done.2, f32[2,2,16,128]{3,2,1,0:T(8,128)S(1)} %copy-done.4, s32[2,2,16]{2,1,0:T(2,128)S(1)} %copy-done.9, f32[19,24,256]{2,1,0:T(8,128)S(1)} %shard_map.119.phi_ref), custom_call_target="tpu_custom_call" | custom-call | flops 1000000 | bytes 1000000 | tf_op jit(solution)/shard_map/pallas_call | solution.py:774
  63.2 30.9 %shard_map.118 = f32[3,2,2,16,128]{4,3,2,1,0:T(8,128)} custom-call(f32[2,4,18,8,128]{4,3,2,1,0:T(8,128)S(1)} %get-tuple-element.28.near2_ref, f32[824,128]{1,0:T(8,128)S(1)} %get-tuple-element.29.own_msg_ref, f32[824,128]{1,0:T(8,128)S(1)} %collective-permute-done.5.got_a_ref, f32[824,128]{1,0:T(8,128)S(1)} %collective-permute-done.6.got_b_ref, ...), custom_call_target="tpu_custom_call" | custom-call | flops 1000000000 | bytes 1000000 | tf_op jit(solution)/shard_map/pallas_call | solution.py:774
  (28 shorter events, 0.1 us)
Async XLA Ops:
  0.6 0.9 copy-start.1
  1.5 0.8 copy-start.3
  2.3 0.7 copy-start.8
  7.1 3.3 %copy-start.11 = (bf16[16,72]{1,0:T(8,128)(2,1)S(1)}, bf16[16,72]{1,0:T(8,128)(2,1)}, u32[]{:S(2)}) copy-start(bf16[16,72]{1,0:T(8,128)(2,1)} %constant.15.clone.down_ref) | copy-start | bytes 6916
  7.1 3.3 %collective-permute-start = (f32[144,128]{1,0:T(8,128)S(1)}, f32[144,128]{1,0:T(8,128)S(1)}, u32[]{:S(2)}, u32[]{:S(2)}) collective-permute-start(f32[144,128]{1,0:T(8,128)S(1)} %get-tuple-element.20.own_msg_ref), channel_id=1, source_target_pairs={{0,1},{1,0},{2,3},{3,2},{4,5},{5,4},{6,7},{7,6},{8,9},{9,8},{10,11... | collective-permute-start | bytes 221192 | tf_op jit(solution)/shard_map/ppermute | solution.py:811
  10.4 1.0 %copy-start = (bf16[2,2,256,256]{3,2,1,0:T(8,128)(2,1)S(1)}, bf16[2,2,256,256]{3,2,1,0:T(8,128)(2,1)}, u32[]{:S(2)}) copy-start(bf16[2,2,256,256]{3,2,1,0:T(8,128)(2,1)} %constant.12.clone.op_ref) | copy-start | bytes 1572868
  11.5 10.5 %copy-start.12 = (s32[2,2,16,128]{3,2,1,0:T(8,128)S(1)}, s32[2,2,16,128]{3,2,1,0:T(8,128)}, u32[]{:S(2)}) copy-start(s32[2,2,16,128]{3,2,1,0:T(8,128)} %refs_2_.3) | copy-start | bytes 98308
  12.6 18.3 %collective-permute-start.2 = (f32[760,128]{1,0:T(8,128)S(1)}, f32[760,128]{1,0:T(8,128)S(1)}, u32[]{:S(2)}, u32[]{:S(2)}) collective-permute-start(f32[760,128]{1,0:T(8,128)S(1)} %get-tuple-element.25), channel_id=1, source_target_pairs={{2,4},{4,2},{6,8},{8,6},{10,12},{12,10},{3,5},{5,3},{7,9},{9,7},{1... | collective-permute-start | bytes 1167368 | tf_op jit(solution)/shard_map/ppermute | solution.py:796
  15.7 20.5 %collective-permute-start.1 = (f32[760,128]{1,0:T(8,128)S(1)}, f32[760,128]{1,0:T(8,128)S(1)}, u32[]{:S(2)}, u32[]{:S(2)}) collective-permute-start(f32[760,128]{1,0:T(8,128)S(1)} %get-tuple-element.24.own_msg_ref), channel_id=1, source_target_pairs={{0,2},{2,0},{4,6},{6,4},{8,10},{10,8},{12,14},{14,12},{1,3},{3,1},... | collective-permute-start | bytes 1167368 | tf_op jit(solution)/shard_map/ppermute | solution.py:796
  17.5 13.3 %collective-permute-start.3 = (f32[152,128]{1,0:T(8,128)S(1)}, f32[152,128]{1,0:T(8,128)S(1)}, u32[]{:S(2)}, u32[]{:S(2)}) collective-permute-start(f32[152,128]{1,0:T(8,128)S(1)} %get-tuple-element.26), channel_id=1, source_target_pairs={{0,4},{4,0},{2,6},{6,2},{8,12},{12,8},{10,14},{14,10},{1,5},{5,1},... | collective-permute-start | bytes 233480 | tf_op jit(solution)/shard_map/ppermute | solution.py:796
  17.5 4.5 %copy-start.9 = (s32[2,2,16]{2,1,0:T(2,128)S(1)}, s32[2,2,16]{2,1,0:T(2,128)}, u32[]{:S(2)}) copy-start(s32[2,2,16]{2,1,0:T(2,128)} %counts_ref.3) | copy-start | bytes 772
  17.5 13.3 %collective-permute-start.4 = (f32[152,128]{1,0:T(8,128)S(1)}, f32[152,128]{1,0:T(8,128)S(1)}, u32[]{:S(2)}, u32[]{:S(2)}) collective-permute-start(f32[152,128]{1,0:T(8,128)S(1)} %get-tuple-element.27), channel_id=1, source_target_pairs={{4,8},{8,4},{6,10},{10,6},{5,9},{9,5},{7,11},{11,7},{20,24},{24,20... | collective-permute-start | bytes 233480 | tf_op jit(solution)/shard_map/ppermute | solution.py:796
  22.0 14.2 %copy-start.6 = (bf16[4,24,168]{2,1,0:T(8,128)(2,1)S(1)}, bf16[4,24,168]{2,1,0:T(8,128)(2,1)}, u32[]{:S(2)}) copy-start(bf16[4,24,168]{2,1,0:T(8,128)(2,1)} %constant.13.clone.fine_ref) | copy-start | bytes 96772
  22.0 14.2 %copy-start.7 = (bf16[4,16,192]{2,1,0:T(8,128)(2,1)S(1)}, bf16[4,16,192]{2,1,0:T(8,128)(2,1)}, u32[]{:S(2)}) copy-start(bf16[4,16,192]{2,1,0:T(8,128)(2,1)} %constant.14.clone.coarse_ref) | copy-start | bytes 73732
  39.8 15.8 %collective-permute-start.6 = (f32[824,128]{1,0:T(8,128)S(1)}, f32[824,128]{1,0:T(8,128)S(1)}, u32[]{:S(2)}, u32[]{:S(2)}) collective-permute-start(f32[824,128]{1,0:T(8,128)S(1)} %get-tuple-element.30), channel_id=1, source_target_pairs={{16,32},{32,16},{48,64},{64,48},{80,96},{96,80},{17,33},{33,17},{4... | collective-permute-start | bytes 1265672 | tf_op jit(solution)/shard_map/ppermute | solution.py:796
  43.0 12.5 %collective-permute-start.5 = (f32[824,128]{1,0:T(8,128)S(1)}, f32[824,128]{1,0:T(8,128)S(1)}, u32[]{:S(2)}, u32[]{:S(2)}) collective-permute-start(f32[824,128]{1,0:T(8,128)S(1)} %get-tuple-element.29.own_msg_ref), channel_id=1, source_target_pairs={{0,16},{16,0},{32,48},{48,32},{64,80},{80,64},{96,112},{112,96},{1... | collective-permute-start | bytes 1265672 | tf_op jit(solution)/shard_map/ppermute | solution.py:796
  43.1 12.4 %collective-permute-start.7 = (f32[48,128]{1,0:T(8,128)S(1)}, f32[48,128]{1,0:T(8,128)S(1)}, u32[]{:S(2)}, u32[]{:S(2)}) collective-permute-start(f32[48,128]{1,0:T(8,128)S(1)} %get-tuple-element.32), channel_id=1, source_target_pairs={{0,32},{32,0},{16,48},{48,16},{64,96},{96,64},{80,112},{112,80},{1... | collective-permute-start | bytes 73736 | tf_op jit(solution)/shard_map/ppermute | solution.py:796
  43.6 11.9 %collective-permute-start.8 = (f32[48,128]{1,0:T(8,128)S(1)}, f32[48,128]{1,0:T(8,128)S(1)}, u32[]{:S(2)}, u32[]{:S(2)}) collective-permute-start(f32[48,128]{1,0:T(8,128)S(1)} %get-tuple-element.33), channel_id=1, source_target_pairs={{32,64},{64,32},{48,80},{80,48},{33,65},{65,33},{49,81},{81,49},{3... | collective-permute-start | bytes 73736 | tf_op jit(solution)/shard_map/ppermute | solution.py:796
  45.7 9.8 %copy-start.5 = (bf16[128,256]{1,0:T(8,128)(2,1)S(1)}, bf16[128,256]{1,0:T(8,128)(2,1)}, u32[]{:S(2)}) copy-start(bf16[128,256]{1,0:T(8,128)(2,1)} %constant.17.clone.up_z_ref) | copy-start | bytes 196612
  45.8 9.8 %copy-start.10 = (bf16[24,48]{1,0:T(8,128)(2,1)S(1)}, bf16[24,48]{1,0:T(8,128)(2,1)}, u32[]{:S(2)}) copy-start(bf16[24,48]{1,0:T(8,128)(2,1)} %constant.16.clone.up_y_ref) | copy-start | bytes 6916
  55.5 1.7 %copy-start.2 = (f32[3,2,2,16,128]{4,3,2,1,0:T(8,128)S(1)}, f32[3,2,2,16,128]{4,3,2,1,0:T(8,128)}, u32[]{:S(2)}) copy-start(f32[3,2,2,16,128]{4,3,2,1,0:T(8,128)} %off_ref.3) | copy-start | bytes 294916
  55.5 1.7 %copy-start.4 = (f32[2,2,16,128]{3,2,1,0:T(8,128)S(1)}, f32[2,2,16,128]{3,2,1,0:T(8,128)}, u32[]{:S(2)}) copy-start(f32[2,2,16,128]{3,2,1,0:T(8,128)} %charge_ref.3) | copy-start | bytes 98308
where the time goes:
time: 95.1 us; the launch traced here: 94.1 us
  Pallas kernels  65.9 us (69%)
  starting transfers between devices  15.6 us (16%)
  waiting for transfers between devices  8.41 us (9%)
  local copies, waits for them, and re-layouts  3.42 us (4%)
    pallas_call x8, Pallas kernels, call(): pl.pallas_call(kernel, out_shape=[jax.ShapeDtypeStruct(s, f32) for s in s...  65.9 us
    ppermute x8, starting transfers between devices, exchange(): lax.ppermute(value, axis, [way for p, q in pairs for way in ((p, q), (q,...  15.3 us
    ppermute x8, waiting for transfers between devices, exchange(): lax.ppermute(value, axis, [way for p, q in pairs for way in ((p, q), (q,...  5.34 us
    unnamed x26, local copies, waits for them, and re-layouts  3.42 us
    ppermute x1, waiting for transfers between devices, per_device(): z_got = lax.ppermute(z_msg, 'ga', [(0, 1), (1, 0)])  3.08 us
  transfers between devices with their start and end apart: 9, of which 2 were waited for; matrix products, arithmetic and copies ran while one was open for 0% of the time, Pallas kernels for 20%

commit v1 on v0

--- a/solution.py
+++ b/solution.py
@@ -10,6 +10,7 @@
 LAST = (((1,), (1,)), ((), ()))
 CAP = 65.0 / 64.0
 TILES = 2
+EARLY = 12
 INNER, OUTER = (128, 8, 4), (64, 16, 1)
 VMEM = pl.BlockSpec(memory_space=pltpu.VMEM)
 SMEM = pl.BlockSpec(memory_space=pltpu.SMEM)
@@ -502,7 +503,7 @@
             packed[tile] = current
             end = end + count
             current = jnp.where((end >> 7) > tile, jnp.where(keep, turned, 0.0), current)
-    start[base + 10] = end
+    start[base + len(levels)] = end
     packed[end >> 7] = jnp.where(lane < (end & 127), current, 0.0)
     for e in range(1, TILES):
         packed[(end >> 7) + e] = jnp.zeros((8, 128), f32)
@@ -649,7 +650,7 @@
     lax.fori_loop(0, cells // 4, finish, 0)
 
 
-def inner_pairs_kernel(part, near_ref, counts_ref, partners_ref, after_ref, out_ref, table, *scratch):
+def inner_pairs_kernel(first, depth, near_ref, counts_ref, partners_ref, after_ref, out_ref, table, *scratch):
     lane = lax.broadcasted_iota(i32, (1, 128), 1)
     for column in range(4):
         table[18 * column] = i32(0)
@@ -662,29 +663,38 @@
 
     lax.fori_loop(0, 16, copy_count, 0)
 
-    levels = [[(near_ref[18 * c + 8 * part + n], table[18 * c + 8 * part + n]) for c in range(4)] for n in range(10)]
-    used = pack_list(scratch[0], scratch[-5], 0, i32(0), levels, 64.0 * part + 40.0)
+    center = 8.0 * first + 4.0 * depth + 8.0
+    levels = [
+        [(near_ref[18 * c + first + n], table[18 * c + first + n]) for c in range(4)] for n in range(depth + 2)
+    ]
+    used = pack_list(scratch[0], scratch[-5], 0, i32(0), levels, center)
+
+    def split(n):
+        column = lax.div(n, i32(depth))
+        return column, n - column * depth
 
     def cell_at(n):
-        return (n >> 3) * 18 + (n & 7) + (8 * part + 1)
+        column, level = split(n)
+        return column * 18 + level + (first + 1)
 
     def emit(n, value, raw):
-        x, y, k = n >> 4, (n >> 3) & 1, 8 * part + (n & 7)
+        column, level = split(n)
+        x, y, k = column >> 1, column & 1, first + level
         count = table[cell_at(n)]
         partner = partners_ref[x, y, pl.ds(k, 1), :]
         other = jnp.take_along_axis(raw, jnp.broadcast_to(partner, (8, 128)), axis=1)
         both = (lane < count) & (partner < count)
-        out_ref[x, y, n & 7, 0:3] = value + jnp.where(both, -0.1 * (raw[0:3] - other[0:3]), 0.0)
+        out_ref[x, y, level, 0:3] = value + jnp.where(both, -0.1 * (raw[0:3] - other[0:3]), 0.0)
 
     pair_sums(
         scratch,
         INNER,
-        32,
+        4 * depth,
         used,
         lambda n: near_ref[cell_at(n)],
         lambda n: table[cell_at(n)],
-        lambda n: n & 7,
-        lambda n: 64.0 * part + 40.0,
+        lambda n: n,
+        lambda n: center,
         emit,
     )
 
@@ -751,9 +761,11 @@
 
     def emit(n, value, raw):
         i, j, part = split(n >> 3)
-        value = value + jnp.where(part == 0, first_ref[i, j, n & 7, 0:3], second_ref[i, j, n & 7, 0:3])
+        k = 8 * part + (n & 7)
+        early = first_ref[i, j, jnp.minimum(k, EARLY - 1), 0:3]
+        value = value + jnp.where(k < EARLY, early, second_ref[i, j, jnp.maximum(k - EARLY, 0), 0:3])
         for d in range(3):
-            out_ref[d, i, j, pl.ds(8 * part + (n & 7), 1), :] = value[d : d + 1]
+            out_ref[d, i, j, pl.ds(k, 1), :] = value[d : d + 1]
 
     pair_sums(
         scratch,
@@ -815,15 +827,15 @@
         (near, rho, z_msg, z_got, z_op, y_down),
     )
     y_got = exchange(y_msgs, "gy")
-    inner = lambda part, near_in, after: call(
-        lambda *refs: inner_pairs_kernel(part, *refs),
-        (2, 2, 8, 8, 128),
+    inner = lambda level, depth, near_in, after: call(
+        lambda *refs: inner_pairs_kernel(level, depth, *refs),
+        (2, 2, depth, 8, 128),
         (near_in.reshape(72, 8, 128), counts, partners, after),
         [VMEM, SMEM, VMEM, ANY],
-        [pltpu.SMEM((72,), i32)] + pair_scratch(INNER, 32, 40 + TILES + 16),
+        [pltpu.SMEM((72,), i32)] + pair_scratch(INNER, 4 * depth, 4 * depth + TILES + 24),
         flops=10**9,
     )
-    first = inner(0, near, full)
+    first = inner(0, EARLY, near, full)
     near2, fine2, _, *x_msgs = call(
         along_y_kernel,
         [(2, 4, 18, 8, 128), (19, 24, 256), (19, 16, 128), (824, 128), (824, 128), (48, 128), (48, 128)],
@@ -831,7 +843,7 @@
         [VMEM] * 10 + [ANY],
     )
     x_got = exchange(x_msgs, "gx")
-    second = inner(1, near, fine2)
+    second = inner(EARLY, 16 - EARLY, near, fine2)
     phi = call(
         along_x_kernel,
         (19, 24, 256),

time: 95.1 us -> 92.2 us (0.970)
  the two profiles are of different devices: /device:TPU:115 before, /device:TPU:10 now
where the time goes in v1:
time: 92.2 us; the launch traced here: 90.8 us
  Pallas kernels  63.8 us (69%)
  starting transfers between devices  20.2 us (22%)
  local copies, waits for them, and re-layouts  3.42 us (4%)
  waiting for transfers between devices  2.45 us (3%)
    pallas_call x8, Pallas kernels, call(): pl.pallas_call(kernel, out_shape=[jax.ShapeDtypeStruct(s, f32) for s in s...  63.8 us
    ppermute x8, starting transfers between devices, exchange(): lax.ppermute(value, axis, [way for p, q in pairs for way in ((p, q), (q,...  18.2 us
    unnamed x26, local copies, waits for them, and re-layouts  3.42 us
    ppermute x1, waiting for transfers between devices, per_device(): z_got = lax.ppermute(z_msg, 'ga', [(0, 1), (1, 0)])  2.43 us
    ppermute x1, starting transfers between devices, per_device(): z_got = lax.ppermute(z_msg, 'ga', [(0, 1), (1, 0)])  2 us
  transfers between devices with their start and end apart: 9, of which 1 were waited for; matrix products, arithmetic and copies ran while one was open for 0% of the time, Pallas kernels for 20%

profile of v1, /device:TPU:10, one launch (start us, length us, event | category | flops | bytes accessed | tf_op | source)
XLA Modules:
  0.0 90.8 jit_solution(4111236402610370412)
XLA Ops:
  0.6 0.9 copy-done.1
  1.5 0.8 copy-done.3
  2.3 0.7 copy-done.8
  3.0 4.1 %shard_map.113 = (f32[2,2,18,8,128]{4,3,2,1,0:T(8,128)S(1)}, f32[19,24,256]{2,1,0:T(8,128)S(1)}, f32[144,128]{1,0:T(8,128)S(1)}) custom-call(f32[3,2,2,16,128]{4,3,2,1,0:T(8,128)S(1)} %copy-done.1, f32[2,2,16,128]{3,2,1,0:T(8,128)S(1)} %copy-done.3, s32[2,2,16]{2,1,0:T(2,128)S(1)} %copy-done.8), custom_call_target="tpu_custom_call" | custom-call | flops 1000000 | bytes 1000000 | tf_op jit(solution)/shard_map/pallas_call | solution.py:786
  7.1 0.0 copy-start.11
  7.1 2.0 %collective-permute-start = (f32[144,128]{1,0:T(8,128)S(1)}, f32[144,128]{1,0:T(8,128)S(1)}, u32[]{:S(2)}, u32[]{:S(2)}) collective-permute-start(f32[144,128]{1,0:T(8,128)S(1)} %get-tuple-element.20.own_msg_ref), channel_id=1, source_target_pairs={{0,1},{1,0},{2,3},{3,2},{4,5},{5,4},{6,7},{7,6},{8,9},{9,8},{10,11... | collective-permute-start | bytes 221192 | tf_op jit(solution)/shard_map/ppermute | solution.py:823
  9.1 2.4 %collective-permute-done.got_ref = f32[144,128]{1,0:T(8,128)S(1)} collective-permute-done((f32[144,128]{1,0:T(8,128)S(1)}, f32[144,128]{1,0:T(8,128)S(1)}, u32[]{:S(2)}, u32[]{:S(2)}) %collective-permute-start) | collective-permute-done | bytes 73760 | tf_op jit(solution)/shard_map/ppermute | solution.py:823
  11.6 1.0 %copy-done = bf16[2,2,256,256]{3,2,1,0:T(8,128)(2,1)S(1)} copy-done((bf16[2,2,256,256]{3,2,1,0:T(8,128)(2,1)S(1)}, bf16[2,2,256,256]{3,2,1,0:T(8,128)(2,1)}, u32[]{:S(2)}) %copy-start) | copy-done | bytes 524312
  12.6 1.1 %shard_map.114 = (f32[2,2,18,8,128]{4,3,2,1,0:T(8,128)S(1)}, f32[19,24,256]{2,1,0:T(8,128)S(1)}, f32[19,16,128]{2,1,0:T(8,128)S(1)}, f32[760,128]{1,0:T(8,128)S(...) custom-call(f32[2,2,18,8,128]{4,3,2,1,0:T(8,128)S(1)} %get-tuple-element.18.near_ref, ...), custom_call_target="tpu_custom_call" | custom-call | flops 1000000 | bytes 1000000 | tf_op jit(solution)/shard_map/pallas_call | solution.py:786
  13.7 5.8 %collective-permute-start.2 = (f32[760,128]{1,0:T(8,128)S(1)}, f32[760,128]{1,0:T(8,128)S(1)}, u32[]{:S(2)}, u32[]{:S(2)}) collective-permute-start(f32[760,128]{1,0:T(8,128)S(1)} %get-tuple-element.25), channel_id=1, source_target_pairs={{2,4},{4,2},{6,8},{8,6},{10,12},{12,10},{3,5},{5,3},{7,9},{9,7},{1... | collective-permute-start | bytes 1167368 | tf_op jit(solution)/shard_map/ppermute | solution.py:808
  19.5 0.7 collective-permute-start.1
  20.2 0.5 collective-permute-start.3
  20.7 4.0 %collective-permute-start.4 = (f32[152,128]{1,0:T(8,128)S(1)}, f32[152,128]{1,0:T(8,128)S(1)}, u32[]{:S(2)}, u32[]{:S(2)}) collective-permute-start(f32[152,128]{1,0:T(8,128)S(1)} %get-tuple-element.27), channel_id=1, source_target_pairs={{4,8},{8,4},{6,10},{10,6},{5,9},{9,5},{7,11},{11,7},{20,24},{24,20... | collective-permute-start | bytes 233480 | tf_op jit(solution)/shard_map/ppermute | solution.py:808
  24.7 0.0 copy-start.6
  24.7 12.6 %shard_map.115.after_ref.first_ref = f32[2,2,12,8,128]{4,3,2,1,0:T(8,128)S(1)} custom-call(f32[72,8,128]{2,1,0:T(8,128)S(1)} %bitcast.1, s32[2,2,16]{2,1,0:T(2,128)S(1)} %copy-done.9, s32[2,2,16,128]{3,2,1,0:T(8,128)S(1)} %copy-done.12, f32[19,24,256]{2,1,0:T(8,128)S(1)} %get-tuple-element.22.refs_3_.full_ref), custom_call_target="tpu_custom_call" | custom-call | flops 1000000000 | bytes 1000000 | tf_op jit(solution)/shard_map/pallas_call | solution.py:786
  37.4 3.6 %shard_map.116 = (f32[2,4,18,8,128]{4,3,2,1,0:T(8,128)S(1)}, f32[19,24,256]{2,1,0:T(8,128)S(1)}, f32[19,16,128]{2,1,0:T(8,128)}, f32[824,128]{1,0:T(8,128)S(1)},...) custom-call(f32[2,2,18,8,128]{4,3,2,1,0:T(8,128)S(1)} %get-tuple-element.21.near1_ref, ...), custom_call_target="tpu_custom_call" | custom-call | flops 1000000 | bytes 1000000 | tf_op jit(solution)/shard_map/pallas_call | solution.py:786
  41.0 1.9 %collective-permute-start.6 = (f32[824,128]{1,0:T(8,128)S(1)}, f32[824,128]{1,0:T(8,128)S(1)}, u32[]{:S(2)}, u32[]{:S(2)}) collective-permute-start(f32[824,128]{1,0:T(8,128)S(1)} %get-tuple-element.30), channel_id=1, source_target_pairs={{16,32},{32,16},{48,64},{64,48},{80,96},{96,80},{17,33},{33,17},{4... | collective-permute-start | bytes 1265672 | tf_op jit(solution)/shard_map/ppermute | solution.py:808
  42.9 2.2 %collective-permute-start.5 = (f32[824,128]{1,0:T(8,128)S(1)}, f32[824,128]{1,0:T(8,128)S(1)}, u32[]{:S(2)}, u32[]{:S(2)}) collective-permute-start(f32[824,128]{1,0:T(8,128)S(1)} %get-tuple-element.29.own_msg_ref), channel_id=1, source_target_pairs={{0,16},{16,0},{32,48},{48,32},{64,80},{80,64},{96,112},{112,96},{1... | collective-permute-start | bytes 1265672 | tf_op jit(solution)/shard_map/ppermute | solution.py:808
  45.2 3.2 %collective-permute-start.8 = (f32[48,128]{1,0:T(8,128)S(1)}, f32[48,128]{1,0:T(8,128)S(1)}, u32[]{:S(2)}, u32[]{:S(2)}) collective-permute-start(f32[48,128]{1,0:T(8,128)S(1)} %get-tuple-element.33), channel_id=1, source_target_pairs={{32,64},{64,32},{48,80},{80,48},{33,65},{65,33},{49,81},{81,49},{3... | collective-permute-start | bytes 73736 | tf_op jit(solution)/shard_map/ppermute | solution.py:808
  48.3 0.0 copy-start.5
  48.4 5.5 %shard_map.117.second_ref.after_ref = f32[2,2,4,8,128]{4,3,2,1,0:T(8,128)S(1)} custom-call(f32[72,8,128]{2,1,0:T(8,128)S(1)} %bitcast.2, s32[2,2,16]{2,1,0:T(2,128)S(1)} %copy-done.9, s32[2,2,16,128]{3,2,1,0:T(8,128)S(1)} %copy-done.12, f32[19,24,256]{2,1,0:T(8,128)S(1)} %get-tuple-element.31.refs_3_.fine2_ref), custom_call_target="tpu_custom_call" | custom-call | flops 1000000000 | bytes 1000000 | tf_op jit(solution)/shard_map/pallas_call | solution.py:786
  54.0 1.6 %shard_map.119.phi_ref = f32[19,24,256]{2,1,0:T(8,128)S(1)} custom-call(f32[19,24,256]{2,1,0:T(8,128)S(1)} %get-tuple-element.31.refs_3_.fine2_ref, f32[824,128]{1,0:T(8,128)S(1)} %get-tuple-element.29.own_msg_ref, f32[824,128]{1,0:T(8,128)S(1)} %collective-permute-done.5.got_a_ref, f32[824,128]{1,0:T(8,128)S(1)} %collective-permute-done.6.got_b_ref, ...), custom_call_target="tpu_custom_call" | custom-call | flops 1000000 | bytes 1000000 | tf_op jit(solution)/shard_map/pallas_call | solution.py:786
  55.6 6.0 %shard_map.120 = f32[3,2,2,16,128]{4,3,2,1,0:T(8,128)} custom-call(f32[3,2,2,16,128]{4,3,2,1,0:T(8,128)S(1)} %copy-done.2, f32[2,2,16,128]{3,2,1,0:T(8,128)S(1)} %copy-done.4, s32[2,2,16]{2,1,0:T(2,128)S(1)} %copy-done.9, f32[19,24,256]{2,1,0:T(8,128)S(1)} %shard_map.119.phi_ref), custom_call_target="tpu_custom_call" | custom-call | flops 1000000 | bytes 1000000 | tf_op jit(solution)/shard_map/pallas_call | solution.py:786
  61.6 29.2 %shard_map.118 = f32[3,2,2,16,128]{4,3,2,1,0:T(8,128)} custom-call(f32[2,4,18,8,128]{4,3,2,1,0:T(8,128)S(1)} %get-tuple-element.28.near2_ref, f32[824,128]{1,0:T(8,128)S(1)} %get-tuple-element.29.own_msg_ref, f32[824,128]{1,0:T(8,128)S(1)} %collective-permute-done.5.got_a_ref, f32[824,128]{1,0:T(8,128)S(1)} %collective-permute-done.6.got_b_ref, ...), custom_call_target="tpu_custom_call" | custom-call | flops 1000000000 | bytes 1000000 | tf_op jit(solution)/shard_map/pallas_call | solution.py:786
  (28 shorter events, 0.1 us)
Async XLA Ops:
  0.6 0.9 copy-start.1
  1.5 0.8 copy-start.3
  2.3 0.7 copy-start.8
  7.1 4.4 %copy-start.11 = (bf16[16,72]{1,0:T(8,128)(2,1)S(1)}, bf16[16,72]{1,0:T(8,128)(2,1)}, u32[]{:S(2)}) copy-start(bf16[16,72]{1,0:T(8,128)(2,1)} %constant.15.clone.down_ref) | copy-start | bytes 6916
  7.1 4.4 %collective-permute-start = (f32[144,128]{1,0:T(8,128)S(1)}, f32[144,128]{1,0:T(8,128)S(1)}, u32[]{:S(2)}, u32[]{:S(2)}) collective-permute-start(f32[144,128]{1,0:T(8,128)S(1)} %get-tuple-element.20.own_msg_ref), channel_id=1, source_target_pairs={{0,1},{1,0},{2,3},{3,2},{4,5},{5,4},{6,7},{7,6},{8,9},{9,8},{10,11... | collective-permute-start | bytes 221192 | tf_op jit(solution)/shard_map/ppermute | solution.py:823
  11.6 1.0 %copy-start = (bf16[2,2,256,256]{3,2,1,0:T(8,128)(2,1)S(1)}, bf16[2,2,256,256]{3,2,1,0:T(8,128)(2,1)}, u32[]{:S(2)}) copy-start(bf16[2,2,256,256]{3,2,1,0:T(8,128)(2,1)} %constant.12.clone.op_ref) | copy-start | bytes 1572868
  12.6 12.1 %copy-start.12 = (s32[2,2,16,128]{3,2,1,0:T(8,128)S(1)}, s32[2,2,16,128]{3,2,1,0:T(8,128)}, u32[]{:S(2)}) copy-start(s32[2,2,16,128]{3,2,1,0:T(8,128)} %refs_2_.3) | copy-start | bytes 98308
  13.7 23.7 %collective-permute-start.2 = (f32[760,128]{1,0:T(8,128)S(1)}, f32[760,128]{1,0:T(8,128)S(1)}, u32[]{:S(2)}, u32[]{:S(2)}) collective-permute-start(f32[760,128]{1,0:T(8,128)S(1)} %get-tuple-element.25), channel_id=1, source_target_pairs={{2,4},{4,2},{6,8},{8,6},{10,12},{12,10},{3,5},{5,3},{7,9},{9,7},{1... | collective-permute-start | bytes 1167368 | tf_op jit(solution)/shard_map/ppermute | solution.py:808
  19.5 17.9 %collective-permute-start.1 = (f32[760,128]{1,0:T(8,128)S(1)}, f32[760,128]{1,0:T(8,128)S(1)}, u32[]{:S(2)}, u32[]{:S(2)}) collective-permute-start(f32[760,128]{1,0:T(8,128)S(1)} %get-tuple-element.24.own_msg_ref), channel_id=1, source_target_pairs={{0,2},{2,0},{4,6},{6,4},{8,10},{10,8},{12,14},{14,12},{1,3},{3,1},... | collective-permute-start | bytes 1167368 | tf_op jit(solution)/shard_map/ppermute | solution.py:808
  20.2 17.2 %collective-permute-start.3 = (f32[152,128]{1,0:T(8,128)S(1)}, f32[152,128]{1,0:T(8,128)S(1)}, u32[]{:S(2)}, u32[]{:S(2)}) collective-permute-start(f32[152,128]{1,0:T(8,128)S(1)} %get-tuple-element.26), channel_id=1, source_target_pairs={{0,4},{4,0},{2,6},{6,2},{8,12},{12,8},{10,14},{14,10},{1,5},{5,1},... | collective-permute-start | bytes 233480 | tf_op jit(solution)/shard_map/ppermute | solution.py:808
  20.7 4.0 %copy-start.9 = (s32[2,2,16]{2,1,0:T(2,128)S(1)}, s32[2,2,16]{2,1,0:T(2,128)}, u32[]{:S(2)}) copy-start(s32[2,2,16]{2,1,0:T(2,128)} %counts_ref.3) | copy-start | bytes 772
  20.7 16.7 %collective-permute-start.4 = (f32[152,128]{1,0:T(8,128)S(1)}, f32[152,128]{1,0:T(8,128)S(1)}, u32[]{:S(2)}, u32[]{:S(2)}) collective-permute-start(f32[152,128]{1,0:T(8,128)S(1)} %get-tuple-element.27), channel_id=1, source_target_pairs={{4,8},{8,4},{6,10},{10,6},{5,9},{9,5},{7,11},{11,7},{20,24},{24,20... | collective-permute-start | bytes 233480 | tf_op jit(solution)/shard_map/ppermute | solution.py:808
  24.7 12.7 %copy-start.6 = (bf16[4,24,168]{2,1,0:T(8,128)(2,1)S(1)}, bf16[4,24,168]{2,1,0:T(8,128)(2,1)}, u32[]{:S(2)}) copy-start(bf16[4,24,168]{2,1,0:T(8,128)(2,1)} %constant.13.clone.fine_ref) | copy-start | bytes 96772
  24.7 12.7 %copy-start.7 = (bf16[4,16,192]{2,1,0:T(8,128)(2,1)S(1)}, bf16[4,16,192]{2,1,0:T(8,128)(2,1)}, u32[]{:S(2)}) copy-start(bf16[4,16,192]{2,1,0:T(8,128)(2,1)} %constant.14.clone.coarse_ref) | copy-start | bytes 73732
  41.0 12.9 %collective-permute-start.6 = (f32[824,128]{1,0:T(8,128)S(1)}, f32[824,128]{1,0:T(8,128)S(1)}, u32[]{:S(2)}, u32[]{:S(2)}) collective-permute-start(f32[824,128]{1,0:T(8,128)S(1)} %get-tuple-element.30), channel_id=1, source_target_pairs={{16,32},{32,16},{48,64},{64,48},{80,96},{96,80},{17,33},{33,17},{4... | collective-permute-start | bytes 1265672 | tf_op jit(solution)/shard_map/ppermute | solution.py:808
  42.9 11.0 %collective-permute-start.5 = (f32[824,128]{1,0:T(8,128)S(1)}, f32[824,128]{1,0:T(8,128)S(1)}, u32[]{:S(2)}, u32[]{:S(2)}) collective-permute-start(f32[824,128]{1,0:T(8,128)S(1)} %get-tuple-element.29.own_msg_ref), channel_id=1, source_target_pairs={{0,16},{16,0},{32,48},{48,32},{64,80},{80,64},{96,112},{112,96},{1... | collective-permute-start | bytes 1265672 | tf_op jit(solution)/shard_map/ppermute | solution.py:808
  45.2 8.8 %collective-permute-start.7 = (f32[48,128]{1,0:T(8,128)S(1)}, f32[48,128]{1,0:T(8,128)S(1)}, u32[]{:S(2)}, u32[]{:S(2)}) collective-permute-start(f32[48,128]{1,0:T(8,128)S(1)} %get-tuple-element.32), channel_id=1, source_target_pairs={{0,32},{32,0},{16,48},{48,16},{64,96},{96,64},{80,112},{112,80},{1... | collective-permute-start | bytes 73736 | tf_op jit(solution)/shard_map/ppermute | solution.py:808
  45.2 8.8 %collective-permute-start.8 = (f32[48,128]{1,0:T(8,128)S(1)}, f32[48,128]{1,0:T(8,128)S(1)}, u32[]{:S(2)}, u32[]{:S(2)}) collective-permute-start(f32[48,128]{1,0:T(8,128)S(1)} %get-tuple-element.33), channel_id=1, source_target_pairs={{32,64},{64,32},{48,80},{80,48},{33,65},{65,33},{49,81},{81,49},{3... | collective-permute-start | bytes 73736 | tf_op jit(solution)/shard_map/ppermute | solution.py:808
  48.3 5.6 %copy-start.5 = (bf16[128,256]{1,0:T(8,128)(2,1)S(1)}, bf16[128,256]{1,0:T(8,128)(2,1)}, u32[]{:S(2)}) copy-start(bf16[128,256]{1,0:T(8,128)(2,1)} %constant.17.clone.up_z_ref) | copy-start | bytes 196612
  48.4 5.6 %copy-start.10 = (bf16[24,48]{1,0:T(8,128)(2,1)S(1)}, bf16[24,48]{1,0:T(8,128)(2,1)}, u32[]{:S(2)}) copy-start(bf16[24,48]{1,0:T(8,128)(2,1)} %constant.16.clone.up_y_ref) | copy-start | bytes 6916
  53.9 1.7 %copy-start.2 = (f32[3,2,2,16,128]{4,3,2,1,0:T(8,128)S(1)}, f32[3,2,2,16,128]{4,3,2,1,0:T(8,128)}, u32[]{:S(2)}) copy-start(f32[3,2,2,16,128]{4,3,2,1,0:T(8,128)} %off_ref.3) | copy-start | bytes 294916
  53.9 1.7 %copy-start.4 = (f32[2,2,16,128]{3,2,1,0:T(8,128)S(1)}, f32[2,2,16,128]{3,2,1,0:T(8,128)}, u32[]{:S(2)}) copy-start(f32[2,2,16,128]{3,2,1,0:T(8,128)} %charge_ref.3) | copy-start | bytes 98308
